TPU v7x, 32 devices: a whole 2x2x4 slice. The times are simulated.
32 devices in a mesh: freq: 4 (over y, x), bond: 8 (over z, core).
Axes of the slice: x: 2, y: 2, z: 4, core: 2. Of those that a mesh axis runs over, the one named last changes fastest.
Arguments:
- gamma: bfloat16 [2, 8, 32, 384, 384], P(None, 'freq', 'bond'), may hold values from -1 to 1
- green: float32 [2, 8, 32, 256], P(None, 'freq', 'bond'), may hold values from -6 to 6
- single: float32 [2, 8, 32, 256], P(None, 'freq', 'bond'), may hold values from -6 to 6
- bond_site: int32 [384], replicated, may hold values from 0 to 255
- causal_mask: int32 [8, 3, 3], P('freq'), may hold values 0 or 1
- site_perm: int32 [384], replicated, may hold values from 0 to 383, each once
Outputs:
- p_vertex: bfloat16 [2, 8, 384, 32, 384], P(None, 'freq', 'bond')
Inputs may be any that keep to these rules, and one draw needn't show every extreme that they name: `bond_site`: each of the 384 bond-Keldysh indices names one site. `causal_mask`: 1 keeps a causality block of 128 x 128 entries, 0 removes it. `site_perm`: a permutation of the 384 column indices.
All inputs are finite; a program needn't handle non-finite values.
Results may differ from a plain program's by a relative error of at most 0.0049.
Values may be sent and summed in bfloat16 or wider, within the bound.
A program may use at most 128 MiB of HBM per device.

v0:
```python
import math
import jax
import jax.numpy as jnp
from jax import lax
from jax.sharding import PartitionSpec as P


def times_complex(first_real, first_imag, second_real, second_imag):
    return (
        first_real * second_real - first_imag * second_imag,
        first_real * second_imag + first_imag * second_real,
    )


def products(pattern, left, right):
    return jnp.einsum(pattern, left, right, preferred_element_type=jnp.float32)


def complex_flow(pattern, left_real, left_imag, gamma_real, gamma_imag):
    flow_real = products(pattern, left_real, gamma_real) - products(pattern, left_imag, gamma_imag)
    flow_imag = products(pattern, left_real, gamma_imag) + products(pattern, left_imag, gamma_real)
    return (flow_real, flow_imag)


def compute_flows(gamma_part, bubble_part, mask_part, site_perm):
    order = gamma_part.shape[-1]
    blocks = mask_part.shape[-1]
    width = order // blocks
    gamma_real = gamma_part[0].astype(jnp.float32)
    gamma_imag = gamma_part[1].astype(jnp.float32)
    bubble_real = bubble_part[0][:, :, None, :]
    bubble_imag = bubble_part[1][:, :, None, :]
    left_real = (gamma_real * bubble_real - gamma_imag * bubble_imag).astype(jnp.bfloat16)
    left_imag = (gamma_real * bubble_imag + gamma_imag * bubble_real).astype(jnp.bfloat16)
    flow_real, flow_imag = complex_flow(
        "wsrk,wskc->wrsc", left_real, left_imag, gamma_part[0], gamma_part[1]
    )
    spread = jnp.repeat(jnp.repeat(mask_part, width, axis=1), width, axis=2).astype(jnp.float32)
    flow_real = flow_real * spread[:, :, None, :]
    flow_imag = flow_imag * spread[:, :, None, :]
    rounded = jnp.stack([flow_real, flow_imag]).astype(jnp.bfloat16)
    return jnp.take(rounded, site_perm, axis=4)


def body(gamma, green, single, bond_site, causal_mask, site_perm):
    local = green.shape[1]
    count = local * lax.axis_size("freq")
    whole_green, whole_single = (
        lax.all_gather(green, "freq", axis=1, tiled=True),
        lax.all_gather(single, "freq", axis=1, tiled=True),
    )
    green_bond = jnp.take(whole_green, bond_site, axis=3)
    single_bond = jnp.take(whole_single, bond_site, axis=3)
    owned = lax.axis_index("freq") * local + jnp.arange(local, dtype=jnp.int32)
    shifts = (jnp.arange(count, dtype=jnp.int32)[None, :] + owned[:, None]) % count
    green_moved = jnp.take(green_bond, shifts, axis=1)
    single_moved = jnp.take(single_bond, shifts, axis=1)
    first = times_complex(
        green_bond[0][None], green_bond[1][None], single_moved[0], single_moved[1]
    )
    second = times_complex(
        single_bond[0][None], single_bond[1][None], green_moved[0], green_moved[1]
    )
    factor = 1.0 / math.sqrt(count)
    bubble = jnp.stack(
        [
            jnp.sum(first[0] + second[0], axis=1) * factor,
            jnp.sum(first[1] + second[1], axis=1) * factor,
        ]
    )
    flows = compute_flows(gamma, bubble, causal_mask, site_perm)
    return lax.all_to_all(flows, "bond", split_axis=2, concat_axis=3, tiled=True)


def solution(mesh):
    in_specs = (
        P(None, "freq", "bond", None, None),
        P(None, "freq", "bond", None),
        P(None, "freq", "bond", None),
        P(),
        P("freq", None, None),
        P(),
    )
    out_specs = P(None, "freq", "bond", None, None)
    return jax.shard_map(body, mesh=mesh, in_specs=in_specs, out_specs=out_specs, check_vma=False)
```

profile of v0, /device:TPU:0, one launch (start us, length us, event | category | flops | bytes accessed | tf_op | source)
XLA Modules:
  0.0 229.6 jit_solution(18322149337392258693)
XLA Ops:
  0.0 0.7 compare_select_fusion
  0.7 0.7 compare_and_fusion.1
  1.5 0.7 copy.95
  2.3 9.7 %all_gather.6 = f32[2,8,4,256]{3,2,0,1:T(4,128)S(1)} all-gather(f32[2,2,4,256]{3,2,0,1:T(4,128)S(1)} %copy.95), channel_id=1, replica_groups=mesh['freq'=4,'bond'=8] {'freq'}, dimensions={1}, use_global_device_ids=true | all-gather | bytes 81920 | tf_op jit(solution)/shard_map/all_gather | solution.py:49
  12.0 0.4 copy.96
  12.4 0.7 copy.98
  13.1 8.2 %all_gather.7 = f32[2,8,4,256]{3,2,0,1:T(4,128)S(1)} all-gather(f32[2,2,4,256]{3,2,0,1:T(4,128)S(1)} %copy.98), channel_id=1, replica_groups=mesh['freq'=4,'bond'=8] {'freq'}, dimensions={1}, use_global_device_ids=true | all-gather | bytes 81920 | tf_op jit(solution)/shard_map/all_gather | solution.py:50
  21.7 3.1 %gather_fusion.1 = f32[384,2,8,4]{2,3,1,0:T(4,128)} fusion(f32[2,8,4,256]{1,2,3,0:T(4,128)S(1)} %copy.96, s32[1024]{0:T(1024)S(1)} %pad_clamp_fusion.2), kind=kCustom, calls=%fused_computation.clone | custom fusion | bytes 198144 | tf_op jit(solution)/shard_map/jit(_take)/gather | solution.py:52
  24.8 3.1 %gather_fusion.2 = f32[384,2,8,4]{2,3,1,0:T(4,128)} fusion(f32[2,8,4,256]{1,2,3,0:T(4,128)S(1)} %copy.99, s32[1024]{0:T(1024)S(1)} %pad_clamp_fusion.2), kind=kCustom, calls=%fused_computation.2.clone | custom fusion | bytes 198144 | tf_op jit(solution)/shard_map/jit(_take)/gather | solution.py:53
  28.0 2.8 %select_bitcast_fusion.2 = (f32[2,8,4,384]{1,2,0,3:T(4,128)S(1)}, f32[2,8,4,384]{1,2,0,3:T(4,128)S(1)}) fusion(f32[384,2,8,4]{2,3,1,0:T(4,128)} %gather_fusion.1, pred[384]{0:T(512)(128)(4,1)S(1)} %compare_and_fusion.1, f32[384,2,8,4]{2,3,1,0:T(4,128)} %gather_fusion.2), kind=kLoop, calls=%fused_computation.40 | loop fusion | flops 49152 | bytes 393600 | tf_op jit(solution)/shard_map/jit(_take)/select_n | solution.py:52
  30.8 0.8 copy.100
  31.5 1.0 copy.104
  32.5 2.0 slice_bitcast_fusion.1
  34.6 0.7 gather_fusion.3
  35.2 0.7 gather_fusion.4
  35.9 1.4 copy.102
  37.3 1.4 copy.103
  38.7 1.4 copy.106
  40.0 1.4 copy.97
  41.7 7.0 %fusion.6 = f32[2,4,384,384]{3,2,1,0:T(8,128)} fusion(f32[2,4,384]{2,1,0:T(4,128)S(1)} %copy_multiply_fusion, f32[2,4,384]{2,1,0:T(4,128)S(1)} %copy_multiply_fusion.1, bf16[2,2,4,384,384]{4,3,2,1,0:T(8,128)(2,1)} %param.10), kind=kOutput, calls=%fused_computation.18 | convolution fusion | flops 913047552 | bytes 11821056 | tf_op jit(solution)/shard_map/wsrk,wskc->wrsc/dot_general | solution.py:16
  48.7 3.8 %fusion.4 = f32[2,4,384,384]{3,2,1,0:T(8,128)} fusion(f32[2,4,384]{2,1,0:T(4,128)S(1)} %copy_multiply_fusion, f32[2,4,384]{2,1,0:T(4,128)S(1)} %copy_multiply_fusion.1, bf16[2,2,4,384,384]{4,3,2,1,0:T(8,128)(2,1)S(1)} %bitcast.115), kind=kOutput, calls=%fused_computation.17 | convolution fusion | flops 913047552 | bytes 11821056 | tf_op jit(solution)/shard_map/wsrk,wskc->wrsc/dot_general | solution.py:16
  53.2 6.1 %fusion.12 = bf16[1,2,384,4,384]{4,2,3,1,0:T(8,128)(2,1)S(1)} fusion(f32[2,4,384,384]{3,2,1,0:T(8,128)} %fusion.6, f32[2,384,384]{2,1,0:T(8,128)S(1)} %copy.111, f32[2,4,384]{2,1,0:T(4,128)S(1)} %copy_multiply_fusion, f32[2,4,384]{2,1,0:T(4,128)S(1)} %copy_multiply_fusion.1, bf16[2,2,4,384,384]{4,3,2,1,0:T(8,128)(2,1)} %param.10), kind=kOutput, calls=%fused_computation.21 | convolution fusion | flops 916586496 | bytes 15360000 | tf_op jit(solution)/shard_map/wsrk,wskc->wrsc/dot_general | solution.py:16
  59.3 6.1 %fusion.13 = bf16[1,2,384,4,384]{4,2,3,1,0:T(8,128)(2,1)S(1)} fusion(f32[2,4,384,384]{3,2,1,0:T(8,128)} %fusion.4, f32[2,384,384]{2,1,0:T(8,128)S(1)} %copy.111, f32[2,4,384]{2,1,0:T(4,128)S(1)} %copy_multiply_fusion, f32[2,4,384]{2,1,0:T(4,128)S(1)} %copy_multiply_fusion.1, bf16[2,2,4,384,384]{4,3,2,1,0:T(8,128)(2,1)} %param.10), kind=kOutput, calls=%fused_computation.22 | convolution fusion | flops 916586496 | bytes 15360000 | tf_op jit(solution)/shard_map/wsrk,wskc->wrsc/dot_general | solution.py:16
  65.4 2.7 %pad_maximum_fusion = bf16[2,2,384,4,384]{4,2,3,1,0:T(8,128)(2,1)} fusion(bf16[1,2,384,4,384]{4,2,3,1,0:T(8,128)(2,1)S(1)} %fusion.13, bf16[1,2,384,4,384]{4,2,3,1,0:T(8,128)(2,1)S(1)} %fusion.12), kind=kLoop, calls=%fused_computation.13 | loop fusion | flops 2359296 | bytes 9437184 | tf_op jit(solution)/shard_map/stack | solution.py:41
  68.1 8.5 %copy.112 = bf16[2,2,384,4,384]{2,3,4,1,0:T(4,128)(2,1)} copy(bf16[2,2,384,4,384]{4,2,3,1,0:T(8,128)(2,1)} %pad_maximum_fusion) | data formatting | bytes 9437184 | tf_op jit(solution)/shard_map/stack | solution.py:41
  76.6 20.7 %gather_fusion = bf16[384,2,2,384,4]{3,4,2,1,0:T(4,128)(2,1)} fusion(bf16[2,2,384,4,384]{2,3,4,1,0:T(4,128)(2,1)} %copy.112, s32[1024]{0:T(1024)S(1)} %pad_clamp_fusion), kind=kCustom, calls=%fused_computation.4 | custom fusion | bytes 9438720 | tf_op jit(solution)/shard_map/jit(_take)/gather | solution.py:42
  97.3 6.8 %select_bitcast_fusion = bf16[2,2,384,4,384]{2,3,1,0,4:T(4,128)(2,1)} fusion(bf16[384,2,2,384,4]{3,4,2,1,0:T(4,128)(2,1)} %gather_fusion, pred[384]{0:T(512)(128)(4,1)S(1)} %compare_and_fusion.2), kind=kLoop, calls=%fused_computation.14 | loop fusion | flops 2359296 | bytes 9437568 | tf_op jit(solution)/shard_map/jit(_take)/select_n | solution.py:42
  104.1 10.3 %copy.113 = bf16[2,2,384,4,384]{4,3,1,0,2:T(4,128)(2,1)} copy(bf16[2,2,384,4,384]{2,3,1,0,4:T(4,128)(2,1)} %select_bitcast_fusion) | data formatting | bytes 9437184 | tf_op jit(solution)/shard_map/jit(_take)/select_n | solution.py:42
  114.4 110.1 %all_to_all.18 = bf16[2,2,384,4,384]{4,3,1,0,2:T(4,128)(2,1)S(1)} all-to-all(bf16[2,2,384,4,384]{4,3,1,0,2:T(4,128)(2,1)} %copy.113), channel_id=1, replica_groups=mesh['freq'=4,'bond'=8] {'bond'}, dimensions={2} | all-to-all | bytes 9437184 | tf_op jit(solution)/shard_map/all_to_all | solution.py:72
  224.5 1.1 copy.114
  225.6 0.8 copy.115
  226.4 3.2 %copy.116 = bf16[2,2,48,32,384]{4,3,2,1,0:T(8,128)(2,1)} copy(bf16[2,2,48,32,384]{4,2,3,1,0:T(8,128)(2,1)S(1)} %bitcast.112) | data formatting | bytes 9437184 | tf_op jit(solution)/shard_map/all_to_all | solution.py:72
  (30 shorter events, 1.6 us)
Async XLA Ops:
  41.5 7.1 %slice-start = ((s8[4718592]{0:T(1024)(128)(4,1)}), s8[4194304]{0:T(1024)(128)(4,1)S(1)}, s32[]{:S(2)}) async-start(s8[4718592]{0:T(1024)(128)(4,1)} %bitcast.114), calls=%async_computation.1 | async-start | bytes 8388608
  41.7 7.0 %slice-start.1 = ((s8[4718592]{0:T(1024)(128)(4,1)}), s8[524288]{0:T(1024)(128)(4,1)S(1)}, s32[]{:S(2)}) async-start(s8[4718592]{0:T(1024)(128)(4,1)} %bitcast.114), calls=%async_computation.2 | async-start | bytes 1048576
  48.7 3.8 %copy-start = (s32[384]{0:T(512)S(1)}, s32[384]{0:T(512)}, u32[]{:S(2)}) copy-start(s32[384]{0:T(512)} %param.15) | copy-start | bytes 4612
  48.7 3.8 %copy-start.1 = (s32[2,3,3]{2,0,1:T(2,128)S(1)}, s32[2,3,3]{2,0,1:T(2,128)}, u32[]{:S(2)}) copy-start(s32[2,3,3]{2,0,1:T(2,128)} %param.14) | copy-start | bytes 220
where the time goes:
time: 231 us; the launch traced here: 230 us
  blocking collectives  128 us (55%)
  local copies, waits for them, and re-layouts  64.3 us (28%)
  matrix products  23 us (10%)
  other arithmetic  14.1 us (6%)
    all_to_all x1, blocking collectives, body(): lax.all_to_all(flows, 'bond', split_axis=2, concat_axis=3, tiled=True)  110 us
    dot_general x4, matrix products, products(): return jnp.einsum(pattern, left, right, preferred_element_type=jnp.float32)  23 us
    gather x1, local copies, waits for them, and re-layouts, compute_flows(): return jnp.take(rounded, site_perm, axis=4)  20.7 us
    select_n x1, local copies, waits for them, and re-layouts, compute_flows(): return jnp.take(rounded, site_perm, axis=4)  10.3 us
    all_gather x1, blocking collectives, body(): lax.all_gather(green, 'freq', axis=1, tiled=True)  9.71 us
    another operation x1, local copies, waits for them, and re-layouts, compute_flows(): rounded = jnp.stack([flow_real, flow_imag]).astype(jnp.bfloat16)  8.47 us
    all_gather x1, blocking collectives, body(): lax.all_gather(single, 'freq', axis=1, tiled=True)  8.2 us
    select_n x2, other arithmetic, compute_flows(): return jnp.take(rounded, site_perm, axis=4)  6.84 us

commit v1 on v0

--- a/solution.py
+++ b/solution.py
@@ -3,6 +3,13 @@
 import jax.numpy as jnp
 from jax import lax
 from jax.sharding import PartitionSpec as P
+
+
+def exchange_blocks(value, axis, split, join):
+    n_dev = lax.axis_size(axis)
+    tiles = jnp.stack(jnp.split(value, n_dev, axis=split), axis=0)
+    tiles = lax.all_to_all(tiles, axis, split_axis=0, concat_axis=0)
+    return jnp.concatenate(tiles, axis=join)
 
 
 def times_complex(first_real, first_imag, second_real, second_imag):
@@ -69,7 +76,7 @@
         ]
     )
     flows = compute_flows(gamma, bubble, causal_mask, site_perm)
-    return lax.all_to_all(flows, "bond", split_axis=2, concat_axis=3, tiled=True)
+    return exchange_blocks(flows, "bond", 2, 3)
 
 
 def solution(mesh):

time: 231 us -> 258 us (1.12)
  local copies, waits for them, and re-layouts: 64.3 us -> 92.3 us
    another operation x0 -> x10, local copies, waits for them, and re-layouts: none -> 34.6 us  [exchange_blocks(): tiles = jnp.stack(jnp.split(value, n_dev, axis=split), axis=0)]
    select_n x1 -> x0, local copies, waits for them, and re-layouts: 10.3 us -> none  [compute_flows(): return jnp.take(rounded, site_perm, axis=4)]
    unnamed x10 -> x23, local copies, waits for them, and re-layouts: 1.47 us -> 6.45 us
    all_to_all x3 -> x1, local copies, waits for them, and re-layouts: 5.12 us -> 0.6 us  [exchange_blocks(): tiles = lax.all_to_all(tiles, axis, split_axis=0, concat_axis=0)]
    reshape x0 -> x1, local copies, waits for them, and re-layouts: none -> 3.21 us  [exchange_blocks(): return jnp.concatenate(tiles, axis=join)]
where the time goes in v1:
time: 258 us; the launch traced here: 257 us
  blocking collectives  128 us (50%)
  local copies, waits for them, and re-layouts  92.3 us (36%)
  matrix products  23 us (9%)
  other arithmetic  13.3 us (5%)
    all_to_all x1, blocking collectives, exchange_blocks(): tiles = lax.all_to_all(tiles, axis, split_axis=0, concat_axis=0)  110 us
    another operation x10, local copies, waits for them, and re-layouts, exchange_blocks(): tiles = jnp.stack(jnp.split(value, n_dev, axis=split), axis=0)  34.6 us
    dot_general x4, matrix products, products(): return jnp.einsum(pattern, left, right, preferred_element_type=jnp.float32)  23 us
    gather x1, local copies, waits for them, and re-layouts, compute_flows(): return jnp.take(rounded, site_perm, axis=4)  20.7 us
    all_gather x1, blocking collectives, body(): lax.all_gather(single, 'freq', axis=1, tiled=True)  9.71 us
    another operation x1, local copies, waits for them, and re-layouts, compute_flows(): rounded = jnp.stack([flow_real, flow_imag]).astype(jnp.bfloat16)  8.46 us
    all_gather x1, blocking collectives, body(): lax.all_gather(green, 'freq', axis=1, tiled=True)  8.21 us
    unnamed x23, local copies, waits for them, and re-layouts  6.45 us

profile of v1, /device:TPU:0, one launch (start us, length us, event | category | flops | bytes accessed | tf_op | source)
XLA Modules:
  0.0 256.7 jit_solution(12801464151597070704)
XLA Ops:
  4.4 9.7 %all_gather.7 = f32[2,8,4,256]{3,2,0,1:T(4,128)S(1)} all-gather(f32[2,2,4,256]{3,2,0,1:T(4,128)S(1)} %copy.66), channel_id=1, replica_groups=mesh['freq'=4,'bond'=8] {'freq'}, dimensions={1}, use_global_device_ids=true | all-gather | bytes 81920 | tf_op jit(solution)/shard_map/all_gather | solution.py:57
  14.1 8.2 %all_gather.6 = f32[2,8,4,256]{3,2,0,1:T(4,128)S(1)} all-gather(f32[2,2,4,256]{3,2,0,1:T(4,128)S(1)} %copy.63), channel_id=1, replica_groups=mesh['freq'=4,'bond'=8] {'freq'}, dimensions={1}, use_global_device_ids=true | all-gather | bytes 81920 | tf_op jit(solution)/shard_map/all_gather | solution.py:56
  23.1 3.1 %gather_fusion.1 = f32[384,2,8,4]{2,3,1,0:T(4,128)} fusion(f32[2,8,4,256]{1,2,3,0:T(4,128)S(1)} %copy.64, s32[1024]{0:T(1024)S(1)} %pad_clamp_fusion.2), kind=kCustom, calls=%fused_computation.clone | custom fusion | bytes 198144 | tf_op jit(solution)/shard_map/jit(_take)/gather | solution.py:59
  26.2 3.2 %gather_fusion.2 = f32[384,2,8,4]{2,3,1,0:T(4,128)} fusion(f32[2,8,4,256]{1,2,3,0:T(4,128)S(1)} %copy.67, s32[1024]{0:T(1024)S(1)} %pad_clamp_fusion.2), kind=kCustom, calls=%fused_computation.2.clone | custom fusion | bytes 198144 | tf_op jit(solution)/shard_map/jit(_take)/gather | solution.py:60
  29.4 2.8 %select_bitcast_fusion.2 = (f32[2,8,4,384]{1,2,0,3:T(4,128)S(1)}, f32[2,8,4,384]{1,2,0,3:T(4,128)S(1)}) fusion(f32[384,2,8,4]{2,3,1,0:T(4,128)} %gather_fusion.1, pred[384]{0:T(512)(128)(4,1)S(1)} %compare_and_fusion.1, f32[384,2,8,4]{2,3,1,0:T(4,128)} %gather_fusion.2), kind=kLoop, calls=%fused_computation.48 | loop fusion | flops 49152 | bytes 393600 | tf_op jit(solution)/shard_map/jit(_take)/select_n | solution.py:59
  33.9 1.9 slice_bitcast_fusion.9
  35.9 1.4 copy.71
  37.3 1.4 copy.74
  38.6 1.4 copy.70
  40.0 1.4 copy.65
  43.1 7.0 %fusion.6 = f32[2,4,384,384]{3,2,1,0:T(8,128)} fusion(f32[2,4,384]{2,1,0:T(4,128)S(1)} %copy_multiply_fusion, f32[2,4,384]{2,1,0:T(4,128)S(1)} %copy_multiply_fusion.1, bf16[2,2,4,384,384]{4,3,2,1,0:T(8,128)(2,1)} %param.10), kind=kOutput, calls=%fused_computation.18 | convolution fusion | flops 913047552 | bytes 11821056 | tf_op jit(solution)/shard_map/wsrk,wskc->wrsc/dot_general | solution.py:23
  50.0 3.8 %fusion.4 = f32[2,4,384,384]{3,2,1,0:T(8,128)} fusion(f32[2,4,384]{2,1,0:T(4,128)S(1)} %copy_multiply_fusion, f32[2,4,384]{2,1,0:T(4,128)S(1)} %copy_multiply_fusion.1, bf16[2,2,4,384,384]{4,3,2,1,0:T(8,128)(2,1)S(1)} %bitcast.129), kind=kOutput, calls=%fused_computation.17 | convolution fusion | flops 913047552 | bytes 11821056 | tf_op jit(solution)/shard_map/wsrk,wskc->wrsc/dot_general | solution.py:23
  54.5 6.1 %fusion.12 = bf16[1,2,384,4,384]{4,2,3,1,0:T(8,128)(2,1)S(1)} fusion(f32[2,4,384,384]{3,2,1,0:T(8,128)} %fusion.6, f32[2,384,384]{2,1,0:T(8,128)S(1)} %copy.79, f32[2,4,384]{2,1,0:T(4,128)S(1)} %copy_multiply_fusion, f32[2,4,384]{2,1,0:T(4,128)S(1)} %copy_multiply_fusion.1, bf16[2,2,4,384,384]{4,3,2,1,0:T(8,128)(2,1)} %param.10), kind=kOutput, calls=%fused_computation.21 | convolution fusion | flops 916586496 | bytes 15360000 | tf_op jit(solution)/shard_map/wsrk,wskc->wrsc/dot_general | solution.py:23
  60.6 6.1 %fusion.13 = bf16[1,2,384,4,384]{4,2,3,1,0:T(8,128)(2,1)S(1)} fusion(f32[2,4,384,384]{3,2,1,0:T(8,128)} %fusion.4, f32[2,384,384]{2,1,0:T(8,128)S(1)} %copy.79, f32[2,4,384]{2,1,0:T(4,128)S(1)} %copy_multiply_fusion, f32[2,4,384]{2,1,0:T(4,128)S(1)} %copy_multiply_fusion.1, bf16[2,2,4,384,384]{4,3,2,1,0:T(8,128)(2,1)} %param.10), kind=kOutput, calls=%fused_computation.22 | convolution fusion | flops 916586496 | bytes 15360000 | tf_op jit(solution)/shard_map/wsrk,wskc->wrsc/dot_general | solution.py:23
  66.7 2.7 %pad_maximum_fusion = bf16[2,2,384,4,384]{4,2,3,1,0:T(8,128)(2,1)} fusion(bf16[1,2,384,4,384]{4,2,3,1,0:T(8,128)(2,1)S(1)} %fusion.13, bf16[1,2,384,4,384]{4,2,3,1,0:T(8,128)(2,1)S(1)} %fusion.12), kind=kLoop, calls=%fused_computation.13 | loop fusion | flops 2359296 | bytes 9437184 | tf_op jit(solution)/shard_map/stack | solution.py:48
  69.4 8.5 %copy.80 = bf16[2,2,384,4,384]{2,3,4,1,0:T(4,128)(2,1)} copy(bf16[2,2,384,4,384]{4,2,3,1,0:T(8,128)(2,1)} %pad_maximum_fusion) | data formatting | bytes 9437184 | tf_op jit(solution)/shard_map/stack | solution.py:48
  77.9 20.7 %gather_fusion = bf16[384,2,2,384,4]{3,4,2,1,0:T(4,128)(2,1)} fusion(bf16[2,2,384,4,384]{2,3,4,1,0:T(4,128)(2,1)} %copy.80, s32[1024]{0:T(1024)S(1)} %get-tuple-element.25), kind=kCustom, calls=%fused_computation.4 | custom fusion | bytes 9438720 | tf_op jit(solution)/shard_map/jit(_take)/gather | solution.py:49
  98.6 4.7 %select_bitcast_fusion = bf16[2,2,384,4,384]{2,3,1,0,4:T(4,128)(2,1)S(1)} fusion(bf16[384,2,2,384,4]{3,4,2,1,0:T(4,128)(2,1)} %gather_fusion, pred[384]{0:T(512)(128)(4,1)S(1)} %compare_and_fusion.2), kind=kLoop, calls=%fused_computation.14 | loop fusion | flops 2359296 | bytes 9437568 | tf_op jit(solution)/shard_map/jit(_take)/select_n | solution.py:49
  103.3 8.0 %slice_bitcast_fusion = (bf16[1,2,2,48,4,384]{3,4,2,1,5,0:T(4,128)(2,1)}, bf16[1,2,2,48,4,384]{3,4,2,1,5,0:T(4,128)(2,1)}, bf16[1,2,2,48,4,384]{3,4,2,1,5,0:T(4,...) fusion(bf16[2,2,384,4,384]{2,3,1,0,4:T(4,128)(2,1)S(1)} %select, ...), kind=kLoop, calls=%fused_computation.39 | loop fusion | bytes 9437184 | tf_op jit(solution)/shard_map/stack | solution.py:10
  111.3 3.7 %copy.88 = bf16[1,2,2,48,4,384]{5,3,4,2,1,0:T(8,128)(2,1)} copy(bf16[1,2,2,48,4,384]{3,4,2,1,5,0:T(4,128)(2,1)} %get-tuple-element.9) | data formatting | bytes 1179648 | tf_op jit(solution)/shard_map/stack | solution.py:10
  115.0 3.7 %copy.87 = bf16[1,2,2,48,4,384]{5,3,4,2,1,0:T(8,128)(2,1)} copy(bf16[1,2,2,48,4,384]{3,4,2,1,5,0:T(4,128)(2,1)} %get-tuple-element.10) | data formatting | bytes 1179648 | tf_op jit(solution)/shard_map/stack | solution.py:10
  118.6 3.7 %copy.86 = bf16[1,2,2,48,4,384]{5,3,4,2,1,0:T(8,128)(2,1)} copy(bf16[1,2,2,48,4,384]{3,4,2,1,5,0:T(4,128)(2,1)} %get-tuple-element.11) | data formatting | bytes 1179648 | tf_op jit(solution)/shard_map/stack | solution.py:10
  122.3 3.7 %copy.85 = bf16[1,2,2,48,4,384]{5,3,4,2,1,0:T(8,128)(2,1)} copy(bf16[1,2,2,48,4,384]{3,4,2,1,5,0:T(4,128)(2,1)} %get-tuple-element.12) | data formatting | bytes 1179648 | tf_op jit(solution)/shard_map/stack | solution.py:10
  126.0 3.7 %copy.84 = bf16[1,2,2,48,4,384]{5,3,4,2,1,0:T(8,128)(2,1)} copy(bf16[1,2,2,48,4,384]{3,4,2,1,5,0:T(4,128)(2,1)} %get-tuple-element.13) | data formatting | bytes 1179648 | tf_op jit(solution)/shard_map/stack | solution.py:10
  129.6 3.7 %copy.83 = bf16[1,2,2,48,4,384]{5,3,4,2,1,0:T(8,128)(2,1)} copy(bf16[1,2,2,48,4,384]{3,4,2,1,5,0:T(4,128)(2,1)} %get-tuple-element.14) | data formatting | bytes 1179648 | tf_op jit(solution)/shard_map/stack | solution.py:10
  133.3 2.3 copy.82
  135.6 2.2 copy.81
  137.8 1.2 constant_dynamic-update-slice_fusion.7
  139.0 1.2 constant_dynamic-update-slice_fusion.6
  140.2 1.2 constant_dynamic-update-slice_fusion.5
  143.0 109.9 %all_to_all.5 = bf16[8,2,2,48,4,384]{5,3,4,2,1,0:T(8,128)(2,1)S(1)} all-to-all(bf16[8,2,2,48,4,384]{5,3,4,2,1,0:T(8,128)(2,1)S(1)} %constant_dynamic-update-slice_fusion), channel_id=1, replica_groups=mesh['freq'=4,'bond'=8] {'bond'}, dimensions={0} | all-to-all | bytes 9437184 | tf_op jit(solution)/shard_map/all_to_all | solution.py:11
  253.5 3.2 %copy.90 = bf16[2,2,48,32,384]{4,3,2,1,0:T(8,128)(2,1)} copy(bf16[2,2,48,32,384]{4,2,3,1,0:T(8,128)(2,1)S(1)} %bitcast.126) | data formatting | bytes 9437184 | tf_op jit(solution)/shard_map/reshape | solution.py:12
  (50 shorter events, 11.4 us)
Async XLA Ops:
  42.9 7.2 %slice-start = ((s8[4718592]{0:T(1024)(128)(4,1)}), s8[4194304]{0:T(1024)(128)(4,1)S(1)}, s32[]{:S(2)}) async-start(s8[4718592]{0:T(1024)(128)(4,1)} %bitcast.128), calls=%async_computation.1 | async-start | bytes 8388608
  43.0 7.0 %slice-start.1 = ((s8[4718592]{0:T(1024)(128)(4,1)}), s8[524288]{0:T(1024)(128)(4,1)S(1)}, s32[]{:S(2)}) async-start(s8[4718592]{0:T(1024)(128)(4,1)} %bitcast.128), calls=%async_computation.2 | async-start | bytes 1048576
  50.0 3.8 %copy-start.4 = (s32[2,3,3]{2,0,1:T(2,128)S(1)}, s32[2,3,3]{2,0,1:T(2,128)}, u32[]{:S(2)}) copy-start(s32[2,3,3]{2,0,1:T(2,128)} %param.14) | copy-start | bytes 220
  135.6 7.1 %copy-start.2 = (bf16[1,2,2,48,4,384]{5,3,4,2,1,0:T(8,128)(2,1)S(1)}, bf16[1,2,2,48,4,384]{5,3,4,2,1,0:T(8,128)(2,1)}, u32[]{:S(2)}) copy-start(bf16[1,2,2,48,4,384]{5,3,4,2,1,0:T(8,128)(2,1)} %copy.86) | copy-start | bytes 1769476
  135.6 7.2 %copy-start.1 = (bf16[1,2,2,48,4,384]{5,3,4,2,1,0:T(8,128)(2,1)S(1)}, bf16[1,2,2,48,4,384]{5,3,4,2,1,0:T(8,128)(2,1)}, u32[]{:S(2)}) copy-start(bf16[1,2,2,48,4,384]{5,3,4,2,1,0:T(8,128)(2,1)} %copy.87) | copy-start | bytes 1769476
  135.6 7.3 %copy-start = (bf16[1,2,2,48,4,384]{5,3,4,2,1,0:T(8,128)(2,1)S(1)}, bf16[1,2,2,48,4,384]{5,3,4,2,1,0:T(8,128)(2,1)}, u32[]{:S(2)}) copy-start(bf16[1,2,2,48,4,384]{5,3,4,2,1,0:T(8,128)(2,1)} %copy.88) | copy-start | bytes 1769476
  137.8 4.7 %copy-start.3 = (bf16[1,2,2,48,4,384]{5,3,4,2,1,0:T(8,128)(2,1)S(1)}, bf16[1,2,2,48,4,384]{5,3,4,2,1,0:T(8,128)(2,1)}, u32[]{:S(2)}) copy-start(bf16[1,2,2,48,4,384]{5,3,4,2,1,0:T(8,128)(2,1)} %copy.85) | copy-start | bytes 1769476
